TPU v7x, 32 devices: a whole 2x2x4 slice. The times are simulated.
32 devices in a mesh: ctx: 8 (over z, x), wsh: 4 (over y, core).
Axes of the slice: x: 2, y: 2, z: 4, core: 2. Of those that a mesh axis runs over, the one named last changes fastest.
Arguments:
- decoder_in: bfloat16 [4, 1536, 512], P('wsh', 'ctx'), may hold values from -6 to 6
- memory: bfloat16 [4, 2048, 512], P('wsh', 'ctx'), may hold values from -6 to 6
- seq_lengths: int32 [4], P('wsh'), may hold values from 384 to 1536, as said below
- mem_lengths: int32 [4], P('wsh'), may hold values from 1024 to 2048, as said below
- self_query: bfloat16 [512, 512], P('wsh'), may hold values from -0.5 to 0.5
- self_keyval: bfloat16 [512, 1024], P('wsh'), may hold values from -0.25 to 0.25
- self_out: bfloat16 [512, 512], P('wsh'), may hold values from -1.25 to 1.25
- cross_query: bfloat16 [512, 512], P('wsh'), may hold values from -0.5 to 0.5
- cross_keyval: bfloat16 [512, 1024], P('wsh'), may hold values from -0.25 to 0.25
- cross_out: bfloat16 [512, 512], P('wsh'), may hold values from -1.5 to 1.5
- ffn_in: bfloat16 [512, 2048], P('wsh'), may hold values from -0.25 to 0.25
- ffn_bias_in: bfloat16 [2048], P('wsh'), may hold values from -3 to 3
- ffn_out: bfloat16 [2048, 512], P('wsh'), may hold values from -0.125 to 0.125
- ffn_bias_out: bfloat16 [512], P('wsh'), may hold values from -3 to 3
- slot_weight: bfloat16 [1024, 512], P('wsh'), may hold values from -0.1875 to 0.1875
- norm_gain: bfloat16 [3, 512], P(None, 'wsh'), may hold values from 0.099609375 to 1.8984375
- norm_bias: bfloat16 [3, 512], P(None, 'wsh'), may hold values from -3 to 3
- cotangent: bfloat16 [4, 1536, 512], P('wsh', 'ctx'), may hold values from -6 to 6
Outputs:
- slots: bfloat16 [4, 1536, 512], P('wsh', 'ctx')
- grad_input: float32 [4, 1536, 512], P('wsh', 'ctx')
- grad_memory: float32 [4, 2048, 512], P('wsh', 'ctx')
- grad_self_query: float32 [512, 512], P('wsh')
- grad_self_keyval: float32 [512, 1024], P('wsh')
- grad_self_out: float32 [512, 512], P('wsh')
- grad_cross_query: float32 [512, 512], P('wsh')
- grad_cross_keyval: float32 [512, 1024], P('wsh')
- grad_cross_out: float32 [512, 512], P('wsh')
- grad_ffn_in: float32 [512, 2048], P('wsh')
- grad_ffn_bias_in: float32 [2048], P('wsh')
- grad_ffn_out: float32 [2048, 512], P('wsh')
- grad_ffn_bias_out: float32 [512], P('wsh')
- grad_slot_weight: float32 [1024, 512], P('wsh')
- grad_norm_gain: float32 [3, 512], P(None, 'wsh')
- grad_norm_bias: float32 [3, 512], P(None, 'wsh')
Inputs may be any that keep to these rules, and one draw needn't show every extreme that they name: `seq_lengths`: some sequence has all 1536 positions live. `mem_lengths`: some sequence has all 2048 memory rows live.
All inputs are finite; a program needn't handle non-finite values.
Results may differ from a plain program's by a relative error of at most 0.034.
The roundings to bfloat16 on the way count: a program that leaves them out, or rounds other values in their place, can miss the bound.
Values may be sent and summed in bfloat16 or wider, within the bound.
No kernel may reach another device: no remote copies, remote signals or barrier semaphores. Data moves between devices by JAX's collectives and lax.ppermute only.
A program may use at most 256 MiB of HBM per device.

v0:
```python
import math
import jax
import jax.numpy as jnp
from jax import lax
from jax.sharding import PartitionSpec as P

HEADS = 8
NORM_EPS = 1e-05
MASK_FILL = -1e30
HIGH = lax.Precision.HIGHEST


def passed_along(shard, axis, by):
    devices = lax.axis_size(axis)
    pairs = [(i, i + by) for i in range(devices) if 0 <= i + by < devices]
    return lax.ppermute(shard, axis, pairs)


def block_rows(n_rows):
    return math.gcd(n_rows, 1024)


def forward_product(left, weight):
    return jnp.dot(left, weight, preferred_element_type=jnp.float32)


def outer_sum(left, right):
    return lax.dot_general(
        left, right, (((0,), (0,)), ((), ())), preferred_element_type=jnp.float32
    )


def back_product(left, weight):
    return lax.dot_general(
        left, weight, (((1,), (1,)), ((), ())), preferred_element_type=jnp.float32
    )


def norm_forward(values, gain_row, bias_row):
    center = values - jnp.mean(values, axis=-1, keepdims=True)
    inverse = lax.rsqrt(jnp.mean(center * center, axis=-1, keepdims=True) + NORM_EPS)
    normed = center * inverse
    return (normed * gain_row + bias_row, normed, inverse)


def norm_backward(grad_out, normed, inverse, gain_row):
    scaled = grad_out * gain_row
    grad_in = inverse * (
        scaled
        - jnp.mean(scaled, axis=-1, keepdims=True)
        - normed * jnp.mean(scaled * normed, axis=-1, keepdims=True)
    )
    return (grad_in, jnp.sum(grad_out * normed, axis=0), jnp.sum(grad_out, axis=0))


def fold_start(n_rows, n_width):
    head_dim = n_width // HEADS
    return (
        jnp.full((HEADS, n_rows), MASK_FILL, jnp.float32),
        jnp.zeros((HEADS, n_rows), jnp.float32),
        jnp.zeros((n_rows, HEADS, head_dim), jnp.float32),
    )


def fold_keys(state, queries, keyvals, first_key, limit):
    n_rows, n_width = queries.shape
    head_dim = n_width // HEADS
    scaling = head_dim ** (-0.5)
    n_keys = keyvals.shape[0]
    stride = block_rows(n_keys)
    query_heads = queries.reshape(n_rows, HEADS, head_dim)
    blocks = keyvals.reshape(n_keys // stride, stride, 2 * n_width)

    def fold_one_block(carry, item):
        running_max, running_sum, weighted = carry
        block, number = item
        key_part = block[:, :n_width].reshape(stride, HEADS, head_dim)
        value_part = block[:, n_width:].reshape(stride, HEADS, head_dim).astype(jnp.float32)
        scores = (
            jnp.einsum("qhd,khd->hqk", query_heads, key_part, preferred_element_type=jnp.float32)
            * scaling
        )
        places = first_key + number * stride + lax.iota(jnp.int32, stride)
        usable = (places < limit)[None, None, :]
        new_max = jnp.maximum(running_max, jnp.max(jnp.where(usable, scores, MASK_FILL), axis=-1))
        powers = jnp.where(usable, jnp.exp(scores - new_max[:, :, None]), 0.0)
        factor = jnp.exp(running_max - new_max)
        running_sum = running_sum * factor + jnp.sum(powers, axis=-1)
        weighted = weighted * factor.T[:, :, None] + jnp.einsum(
            "hqk,khd->qhd", powers, value_part, precision=HIGH, preferred_element_type=jnp.float32
        )
        return ((new_max, running_sum, weighted), None)

    numbers = jnp.arange(n_keys // stride, dtype=jnp.int32)
    state, unused = lax.scan(fold_one_block, state, (blocks, numbers))
    return state


def fold_finish(state):
    running_max, running_sum, weighted = state
    n_rows = weighted.shape[0]
    mixed = (weighted / running_sum.T[:, :, None]).reshape(n_rows, -1)
    return (mixed, running_max + jnp.log(running_sum))


def row_delta(grad_low, mixed):
    n_rows = mixed.shape[0]
    return jnp.sum((grad_low.astype(jnp.float32) * mixed).reshape(n_rows, HEADS, -1), axis=-1).T


def attend_back(queries, grad_out, log_sums, deltas, keyvals, limit):
    n_rows, n_width = queries.shape
    head_dim = n_width // HEADS
    scaling = head_dim ** (-0.5)
    n_keys = keyvals.shape[0]
    stride = block_rows(n_keys)
    query_heads = queries.reshape(n_rows, HEADS, head_dim)
    grad_heads = grad_out.reshape(n_rows, HEADS, head_dim)
    grad_wide = grad_heads.astype(jnp.float32)
    blocks = keyvals.reshape(n_keys // stride, stride, 2 * n_width)

    def attend_one_block(carry, item):
        block, number = item
        key_part = block[:, :n_width].reshape(stride, HEADS, head_dim)
        value_part = block[:, n_width:].reshape(stride, HEADS, head_dim)
        scores = (
            jnp.einsum("qhd,khd->hqk", query_heads, key_part, preferred_element_type=jnp.float32)
            * scaling
        )
        places = number * stride + lax.iota(jnp.int32, stride)
        usable = (places < limit)[None, None, :]
        probs = jnp.where(usable, jnp.exp(scores - log_sums[:, :, None]), 0.0)
        d_probs = jnp.einsum(
            "qhd,khd->hqk", grad_heads, value_part, preferred_element_type=jnp.float32
        )
        d_scores = (probs * (d_probs - deltas[:, :, None])).astype(jnp.bfloat16)
        carry = (
            carry
            + jnp.einsum("hqk,khd->qhd", d_scores, key_part, preferred_element_type=jnp.float32)
            * scaling
        )
        d_keys = (
            jnp.einsum("hqk,qhd->khd", d_scores, query_heads, preferred_element_type=jnp.float32)
            * scaling
        )
        d_values = jnp.einsum(
            "hqk,qhd->khd", probs, grad_wide, precision=HIGH, preferred_element_type=jnp.float32
        )
        return (
            carry,
            jnp.concatenate(
                [d_keys.reshape(stride, n_width), d_values.reshape(stride, n_width)], axis=1
            ),
        )

    numbers = jnp.arange(n_keys // stride, dtype=jnp.int32)
    start_grad = jnp.zeros((n_rows, HEADS, head_dim), jnp.float32)
    d_query, key_terms = lax.scan(attend_one_block, start_grad, (blocks, numbers))
    return (d_query.reshape(n_rows, n_width), key_terms.reshape(n_keys, 2 * n_width))


def shards(
    decoder_in,
    memory,
    seq_lengths,
    mem_lengths,
    self_query,
    self_keyval,
    self_out,
    cross_query,
    cross_keyval,
    cross_out,
    ffn_in,
    ffn_bias_in,
    ffn_out,
    ffn_bias_out,
    slot_weight,
    norm_gain,
    norm_bias,
    cotangent,
):
    gathered = (
        lax.all_gather(self_query, "wsh", axis=0, tiled=True),
        lax.all_gather(self_keyval, "wsh", axis=0, tiled=True),
        lax.all_gather(self_out, "wsh", axis=0, tiled=True),
        lax.all_gather(cross_query, "wsh", axis=0, tiled=True),
        lax.all_gather(cross_keyval, "wsh", axis=0, tiled=True),
        lax.all_gather(cross_out, "wsh", axis=0, tiled=True),
        lax.all_gather(ffn_in, "wsh", axis=0, tiled=True),
        lax.all_gather(ffn_bias_in, "wsh", axis=0, tiled=True),
        lax.all_gather(ffn_out, "wsh", axis=0, tiled=True),
        lax.all_gather(ffn_bias_out, "wsh", axis=0, tiled=True),
        lax.all_gather(slot_weight, "wsh", axis=0, tiled=True),
        lax.all_gather(norm_gain, "wsh", axis=1, tiled=True),
        lax.all_gather(norm_bias, "wsh", axis=1, tiled=True),
    )
    (
        w_query,
        w_keyval,
        w_out,
        c_query,
        c_keyval,
        c_out,
        w_first,
        b_first,
        w_second,
        b_second,
        w_slot,
        gains,
        biases,
    ) = gathered
    tokens = decoder_in[0]
    n_rows, n_width = tokens.shape
    live_count = seq_lengths[0]
    mem_count = mem_lengths[0]
    places = lax.axis_index("ctx") * n_rows + lax.iota(jnp.int32, n_rows)
    live = (places < live_count)[:, None]
    valid = live.astype(jnp.float32)
    gains = gains.astype(jnp.float32)
    biases = biases.astype(jnp.float32)
    queries = forward_product(tokens, w_query).astype(jnp.bfloat16)
    keyvals = forward_product(tokens, w_keyval).astype(jnp.bfloat16)
    self_state = fold_keys(
        fold_start(n_rows, n_width),
        queries,
        lax.all_gather(keyvals, "ctx", axis=0, tiled=True),
        jnp.int32(0),
        live_count,
    )
    self_mixed, self_lse = fold_finish(self_state)
    self_low = self_mixed.astype(jnp.bfloat16)
    first_sum = tokens.astype(jnp.float32) + forward_product(self_low, w_out)
    hidden_one, normed_one, inverse_one = norm_forward(first_sum, gains[0], biases[0])
    hidden_one_low = hidden_one.astype(jnp.bfloat16)
    cross_queries = forward_product(hidden_one_low, c_query).astype(jnp.bfloat16)
    mem_rows = memory[0]
    mem_keyvals = forward_product(mem_rows, c_keyval).astype(jnp.bfloat16)
    mem_all = lax.all_gather(mem_keyvals, "ctx", axis=0, tiled=True)
    cross_state = fold_keys(fold_start(n_rows, n_width), cross_queries, mem_all, 0, mem_count)
    cross_mixed, cross_lse = fold_finish(cross_state)
    cross_low = cross_mixed.astype(jnp.bfloat16)
    second_sum = hidden_one + forward_product(cross_low, c_out)
    hidden_two, normed_two, inverse_two = norm_forward(second_sum, gains[1], biases[1])
    hidden_two_low = hidden_two.astype(jnp.bfloat16)
    preact = forward_product(hidden_two_low, w_first) + b_first.astype(jnp.float32)
    active_wide, gelu_pull = jax.vjp(jax.nn.gelu, preact)
    active = active_wide.astype(jnp.bfloat16)
    third_sum = hidden_two + forward_product(active, w_second) + b_second.astype(jnp.float32)
    hidden_three, normed_three, inverse_three = norm_forward(third_sum, gains[2], biases[2])
    masked_low = (hidden_three * valid).astype(jnp.bfloat16)
    next_row = passed_along(masked_low[:1], "ctx", -1)
    paired = jnp.concatenate(
        [masked_low, jnp.concatenate([masked_low[1:], next_row], axis=0)], axis=1
    )
    slots = (forward_product(paired, w_slot) * valid).astype(jnp.bfloat16)
    grad_slots = jnp.where(live, cotangent[0], jnp.zeros_like(cotangent[0]))
    g_slot = outer_sum(paired, grad_slots)
    d_paired = back_product(grad_slots, w_slot)
    d_own = d_paired[:, :n_width]
    d_next = d_paired[:, n_width:]
    carried = passed_along(d_next[-1:], "ctx", 1)
    d_three = (d_own + jnp.concatenate([carried, d_next[:-1]], axis=0)) * valid
    d_third, g_gain_three, g_bias_three = norm_backward(
        d_three, normed_three, inverse_three, gains[2]
    )
    e_third = d_third.astype(jnp.bfloat16)
    g_second = outer_sum(active, e_third)
    g_bsecond = jnp.sum(e_third.astype(jnp.float32), axis=0)
    d_pre = gelu_pull(back_product(e_third, w_second))[0].astype(jnp.bfloat16)
    g_bfirst = jnp.sum(d_pre.astype(jnp.float32), axis=0)
    g_first = outer_sum(hidden_two_low, d_pre)
    d_two = d_third + back_product(d_pre, w_first)
    d_second, g_gain_two, g_bias_two = norm_backward(d_two, normed_two, inverse_two, gains[1])
    e_second = d_second.astype(jnp.bfloat16)
    g_cout = outer_sum(cross_low, e_second)
    d_cross = back_product(e_second, c_out).astype(jnp.bfloat16)
    d_cq, mem_terms = attend_back(
        cross_queries, d_cross, cross_lse, row_delta(d_cross, cross_mixed), mem_all, mem_count
    )
    d_memkv = lax.psum_scatter(mem_terms, "ctx", scatter_dimension=0, tiled=True).astype(
        jnp.bfloat16
    )
    g_ckv = outer_sum(mem_rows, d_memkv)
    grad_memory = back_product(d_memkv, c_keyval)
    d_cq_low = d_cq.astype(jnp.bfloat16)
    g_cquery = outer_sum(hidden_one_low, d_cq_low)
    d_one = d_second + back_product(d_cq_low, c_query)
    d_first, g_gain_one, g_bias_one = norm_backward(d_one, normed_one, inverse_one, gains[0])
    e_first = d_first.astype(jnp.bfloat16)
    g_out = outer_sum(self_low, e_first)
    d_self = back_product(e_first, w_out).astype(jnp.bfloat16)
    keyval_back = lax.all_gather(keyvals, "ctx", axis=0, tiled=True)
    self_delta = row_delta(d_self, self_mixed)
    d_query, key_terms = attend_back(queries, d_self, self_lse, self_delta, keyval_back, live_count)
    d_kv = lax.psum_scatter(key_terms, "ctx", scatter_dimension=0, tiled=True).astype(jnp.bfloat16)
    d_query_low = d_query.astype(jnp.bfloat16)
    g_query = outer_sum(tokens, d_query_low)
    g_keyval = outer_sum(tokens, d_kv)
    grad_input = d_first + back_product(d_query_low, w_query) + back_product(d_kv, w_keyval)
    g_gains = jnp.stack([g_gain_one, g_gain_two, g_gain_three])
    g_biases = jnp.stack([g_bias_one, g_bias_two, g_bias_three])
    summed = lax.psum(
        (
            g_query,
            g_keyval,
            g_out,
            g_cquery,
            g_ckv,
            g_cout,
            g_first,
            g_bfirst,
            g_second,
            g_bsecond,
            g_slot,
            g_gains,
            g_biases,
        ),
        "ctx",
    )
    shares = (
        lax.psum_scatter(
            summed[0].astype(jnp.bfloat16), "wsh", scatter_dimension=0, tiled=True
        ).astype(jnp.float32),
        lax.psum_scatter(
            summed[1].astype(jnp.bfloat16), "wsh", scatter_dimension=0, tiled=True
        ).astype(jnp.float32),
        lax.psum_scatter(
            summed[2].astype(jnp.bfloat16), "wsh", scatter_dimension=0, tiled=True
        ).astype(jnp.float32),
        lax.psum_scatter(
            summed[3].astype(jnp.bfloat16), "wsh", scatter_dimension=0, tiled=True
        ).astype(jnp.float32),
        lax.psum_scatter(
            summed[4].astype(jnp.bfloat16), "wsh", scatter_dimension=0, tiled=True
        ).astype(jnp.float32),
        lax.psum_scatter(
            summed[5].astype(jnp.bfloat16), "wsh", scatter_dimension=0, tiled=True
        ).astype(jnp.float32),
        lax.psum_scatter(
            summed[6].astype(jnp.bfloat16), "wsh", scatter_dimension=0, tiled=True
        ).astype(jnp.float32),
        lax.psum_scatter(
            summed[7].astype(jnp.bfloat16), "wsh", scatter_dimension=0, tiled=True
        ).astype(jnp.float32),
        lax.psum_scatter(
            summed[8].astype(jnp.bfloat16), "wsh", scatter_dimension=0, tiled=True
        ).astype(jnp.float32),
        lax.psum_scatter(
            summed[9].astype(jnp.bfloat16), "wsh", scatter_dimension=0, tiled=True
        ).astype(jnp.float32),
        lax.psum_scatter(
            summed[10].astype(jnp.bfloat16), "wsh", scatter_dimension=0, tiled=True
        ).astype(jnp.float32),
        lax.psum_scatter(
            summed[11].astype(jnp.bfloat16), "wsh", scatter_dimension=1, tiled=True
        ).astype(jnp.float32),
        lax.psum_scatter(
            summed[12].astype(jnp.bfloat16), "wsh", scatter_dimension=1, tiled=True
        ).astype(jnp.float32),
    )
    return (
        slots[None],
        grad_input[None],
        grad_memory[None],
        shares[0],
        shares[1],
        shares[2],
        shares[3],
        shares[4],
        shares[5],
        shares[6],
        shares[7],
        shares[8],
        shares[9],
        shares[10],
        shares[11],
        shares[12],
    )


def solution(mesh):
    in_specs = (
        P("wsh", "ctx", None),
        P("wsh", "ctx", None),
        P("wsh"),
        P("wsh"),
        P("wsh", None),
        P("wsh", None),
        P("wsh", None),
        P("wsh", None),
        P("wsh", None),
        P("wsh", None),
        P("wsh", None),
        P("wsh"),
        P("wsh", None),
        P("wsh"),
        P("wsh", None),
        P(None, "wsh"),
        P(None, "wsh"),
        P("wsh", "ctx", None),
    )
    out_specs = (
        P("wsh", "ctx", None),
        P("wsh", "ctx", None),
        P("wsh", "ctx", None),
        P("wsh", None),
        P("wsh", None),
        P("wsh", None),
        P("wsh", None),
        P("wsh", None),
        P("wsh", None),
        P("wsh", None),
        P("wsh"),
        P("wsh", None),
        P("wsh"),
        P("wsh", None),
        P(None, "wsh"),
        P(None, "wsh"),
    )
    return jax.shard_map(shards, mesh=mesh, in_specs=in_specs, out_specs=out_specs, check_vma=False)
```

profile of v0, /device:TPU:0, one launch (start us, length us, event | category | flops | bytes accessed | tf_op | source)
XLA Modules:
  0.0 1701.6 jit_solution(16746929962556680504)
XLA Ops:
  9.5 19.6 %all-gather.10.cloned.1.call-done = bf16[512,1024]{1,0:T(8,128)(2,1)} async-done(((bf16[128,1024]{1,0:T(8,128)(2,1)}), bf16[512,1024]{1,0:T(8,128)(2,1)}) %all-gather.10.cloned.1.call-update) | async-done | bytes 1048592 | tf_op jit(solution)/shard_map/all_gather | solution.py:184
  31.6 15.8 all-gather.14.cloned.1.call-done
  63.4 7.7 all_gather.55
  71.1 7.7 all_gather.54
  78.8 7.7 all_gather.49
  115.4 13.5 all-gather.12.cloned.1.call-done
  133.5 27.7 %while.56 = (s32[]{:T(128)}, f32[8,192]{1,0:T(8,128)S(1)}, f32[8,192]{1,0:T(8,128)S(1)}, f32[192,8,64]{0,2,1:T(8,128)}, s32[3]{0:T(128)S(1)}, /*index=5*/s32[]{:...) while((s32[]{:T(128)}, f32[8,192]{1,0:T(8,128)S(1)}, ...), condition=%wide.region_3.4_spmd.clone, body=%wide.region_0.3_spmd.clone.sunk | while | flops 712812544 | bytes 21793044 | solution.py:95
  166.4 37.1 %all-gather.16.cloned.1.call-done = bf16[2048,1024]{1,0:T(8,128)(2,1)} async-done(((bf16[256,1024]{1,0:T(8,128)(2,1)}), bf16[2048,1024]{1,0:T(8,128)(2,1)}) %all-gather.16.cloned.1.call-update) | async-done | bytes 4194320 | tf_op jit(solution)/shard_map/all_gather | solution.py:238
  209.8 34.2 %while.57 = (s32[]{:T(128)}, f32[8,192]{1,0:T(8,128)S(1)}, f32[8,192]{1,0:T(8,128)S(1)}, f32[192,8,64]{0,2,1:T(8,128)S(1)}, s32[2]{0:T(128)S(1)}, /*index=5*/s32...) while((s32[]{:T(128)}, f32[8,192]{1,0:T(8,128)S(1)}, ...), condition=%wide.region_9.10_spmd.clone, body=%wide.region_6.9_spmd.clone.sunk | while | flops 1425320960 | bytes 55611584 | solution.py:95
  268.1 67.6 %while.58 = (s32[]{:T(128)}, f32[192,8,64]{0,2,1:T(8,128)}, f32[2,1024,1024]{2,1,0:T(8,128)}, bf16[2,1024,1024]{1,2,0:T(8,128)(2,1)}, s32[2]{0:T(128)S(1)}, /*in...) while((s32[]{:T(128)}, f32[192,8,64]{0,2,1:T(8,128)}, ...), condition=%wide.region_20.21_spmd.clone, body=%wide.region_19.20_spmd.clone.sunk | while | flops 2029291520 | bytes 105100704 | solution.py:158
  344.5 57.7 %while.59 = (s32[]{:T(128)}, f32[192,8,64]{0,2,1:T(8,128)}, f32[3,512,1024]{2,1,0:T(8,128)}, bf16[3,512,1024]{1,2,0:T(8,128)(2,1)}, s32[3]{0:T(128)S(1)}, /*inde...) while((s32[]{:T(128)}, f32[192,8,64]{0,2,1:T(8,128)}, ...), condition=%wide.region_25.26_spmd.clone, body=%wide.region_24.25_spmd.clone.sunk | while | flops 1014793216 | bytes 47927116 | solution.py:158
  418.7 101.6 %reduce-scatter.24.cloned.1.call-done = f32[192,1024]{1,0:T(8,128)} async-done(((f32[1536,1024]{1,0:T(8,128)}), f32[192,1024]{1,0:T(8,128)}) %reduce-scatter.24.cloned.1.call-update) | async-done | bytes 786448 | tf_op jit(solution)/shard_map/reduce_scatter | solution.py:295
  523.3 148.9 %reduce-scatter.26.cloned.1.call-done = f32[256,1024]{1,0:T(8,128)} async-done(((f32[2048,1024]{1,0:T(8,128)}), f32[256,1024]{1,0:T(8,128)}) %reduce-scatter.26.cloned.1.call-update) | async-done | bytes 1048592 | tf_op jit(solution)/shard_map/reduce_scatter | solution.py:280
  675.3 726.0 %all-reduce.5 = (bf16[512,512]{0,1:T(8,128)(2,1)}, bf16[512,1024]{0,1:T(8,128)(2,1)}, bf16[512,1024]{0,1:T(8,128)(2,1)}, bf16[512,512]{1,0:T(8,128)(2,1)}, bf16[...) all-reduce(f32[512,512]{0,1:T(8,128)} %convolution_bitcast_fusion.2, ...), channel_id=1, replica_groups=mesh['ctx'=8,'wsh'=4] {'ctx'}, use_global_device_ids=true, to_apply=%region_28.29 | all-reduce | flops 4724224 | bytes 28345344 | tf_op jit(solution)/shard_map/psum | solution.py:302
  1430.5 12.7 reduce-scatter.48.cloned.1.call-done
  1444.6 22.8 %reduce-scatter.40.cloned.1.call-done = bf16[128,512]{1,0:T(8,128)(2,1)} async-done(((bf16[512,512]{1,0:T(8,128)(2,1)}), bf16[128,512]{1,0:T(8,128)(2,1)}) %reduce-scatter.40.cloned.1.call-update) | async-done | bytes 131088
  1469.3 22.9 %reduce-scatter.28.cloned.1.call-done = bf16[128,512]{1,0:T(8,128)(2,1)} async-done(((bf16[512,512]{1,0:T(8,128)(2,1)}), bf16[128,512]{1,0:T(8,128)(2,1)}) %reduce-scatter.28.cloned.1.call-update) | async-done | bytes 131088 | tf_op jit(solution)/shard_map/reduce_scatter | solution.py:327
  1493.8 23.2 %reduce-scatter.30.cloned.1.call-done = bf16[128,512]{1,0:T(8,128)(2,1)} async-done(((bf16[512,512]{1,0:T(8,128)(2,1)}), bf16[128,512]{1,0:T(8,128)(2,1)}) %reduce-scatter.30.cloned.1.call-update) | async-done | bytes 131088 | tf_op jit(solution)/shard_map/reduce_scatter | solution.py:330
  1518.6 22.4 %reduce-scatter.32.cloned.1.call-done = bf16[128,512]{1,0:T(8,128)(2,1)} async-done(((bf16[512,512]{1,0:T(8,128)(2,1)}), bf16[128,512]{1,0:T(8,128)(2,1)}) %reduce-scatter.32.cloned.1.call-update) | async-done | bytes 131088 | tf_op jit(solution)/shard_map/reduce_scatter | solution.py:336
  1542.6 26.4 %reduce-scatter.42.cloned.1.call-done = bf16[128,1024]{1,0:T(8,128)(2,1)} async-done(((bf16[512,1024]{1,0:T(8,128)(2,1)}), bf16[128,1024]{1,0:T(8,128)(2,1)}) %reduce-scatter.42.cloned.1.call-update) | async-done | bytes 262160
  1571.1 25.8 %reduce-scatter.44.cloned.1.call-done = bf16[128,1024]{1,0:T(8,128)(2,1)} async-done(((bf16[512,1024]{1,0:T(8,128)(2,1)}), bf16[128,1024]{1,0:T(8,128)(2,1)}) %reduce-scatter.44.cloned.1.call-update) | async-done | bytes 262160
  1599.0 25.4 %reduce-scatter.38.cloned.1.call-done = bf16[256,512]{1,0:T(8,128)(2,1)} async-done(((bf16[1024,512]{1,0:T(8,128)(2,1)}), bf16[256,512]{1,0:T(8,128)(2,1)}) %reduce-scatter.38.cloned.1.call-update) | async-done | bytes 262160 | tf_op jit(solution)/shard_map/reduce_scatter | solution.py:351
  1626.2 32.1 %reduce-scatter.34.cloned.1.call-done = bf16[128,2048]{1,0:T(8,128)(2,1)} async-done(((bf16[512,2048]{1,0:T(8,128)(2,1)}), bf16[128,2048]{1,0:T(8,128)(2,1)}) %reduce-scatter.34.cloned.1.call-update) | async-done | bytes 524304 | tf_op jit(solution)/shard_map/reduce_scatter | solution.py:339
  1660.4 31.9 %reduce-scatter.36.cloned.1.call-done = bf16[512,512]{1,0:T(8,128)(2,1)} async-done(((bf16[2048,512]{1,0:T(8,128)(2,1)}), bf16[512,512]{1,0:T(8,128)(2,1)}) %reduce-scatter.36.cloned.1.call-update) | async-done | bytes 524304 | tf_op jit(solution)/shard_map/reduce_scatter | solution.py:345
  (541 shorter events, 344.8 us)
Async XLA Ops:
  7.2 21.9 %all-gather.10.cloned.1.call-start = ((), (), s32[]{:S(2)}) async-start(), calls=%async_computation.13 | async-start | bytes 1310720 | tf_op jit(solution)/shard_map/all_gather | solution.py:184
  8.0 39.4 %all-gather.14.cloned.1.call-start = ((), (), s32[]{:S(2)}) async-start(), calls=%async_computation.15 | async-start | bytes 1310720 | tf_op jit(solution)/shard_map/all_gather | solution.py:187
  8.7 98.9 %all-gather.22.cloned.1.call-start = ((), (), s32[]{:S(2)}) async-start(), calls=%async_computation.19 | async-start | bytes 1310720 | tf_op jit(solution)/shard_map/all_gather | solution.py:193
  9.5 119.4 %all-gather.12.cloned.1.call-start = ((), (), s32[]{:S(2)}) async-start(), calls=%async_computation.14 | async-start | bytes 3538944 | tf_op jit(solution)/shard_map/all_gather | solution.py:226
  31.6 171.9 %all-gather.16.cloned.1.call-start = ((), (), s32[]{:S(2)}) async-start(), calls=%async_computation.16 | async-start | bytes 4718592 | tf_op jit(solution)/shard_map/all_gather | solution.py:238
  49.9 195.5 %all-gather.18.cloned.1.call-start = ((), (), s32[]{:S(2)}) async-start(), calls=%async_computation.17 | async-start | bytes 2621440 | tf_op jit(solution)/shard_map/all_gather | solution.py:189
  50.5 199.6 %all-gather.20.cloned.1.call-start = ((), (), s32[]{:S(2)}) async-start(), calls=%async_computation.18 | async-start | bytes 2621440 | tf_op jit(solution)/shard_map/all_gather | solution.py:191
  51.2 469.2 %reduce-scatter.24.cloned.1.call-start = ((), (), s32[]{:S(2)}) async-start(), calls=%async_computation.20 | async-start | bytes 7077888 | tf_op jit(solution)/shard_map/reduce_scatter | solution.py:295
  110.9 144.0 %collective-permute-start.1 = (f32[1,512]{1,0:T(1,128)}, f32[1,512]{1,0:T(1,128)}, u32[]{:S(2)}, u32[]{:S(2)}) collective-permute-start(f32[1,512]{1,0:T(1,128)} %slice.99), channel_id=1, source_target_pairs={{0,4},{4,8},{8,12},{12,16},{16,20},{20,24},{24,28},{1,5},{5,9},{9,... | collective-permute-start | bytes 6152 | tf_op jit(solution)/shard_map/ppermute | solution.py:16
  402.2 269.9 %reduce-scatter.26.cloned.1.call-start = ((), (), s32[]{:S(2)}) async-start(), calls=%async_computation.21 | async-start | bytes 9437184 | tf_op jit(solution)/shard_map/reduce_scatter | solution.py:280
  403.0 1026.0 %reduce-scatter.46.cloned.1.call-start = ((), (), s32[]{:S(2)}) async-start(), calls=%async_computation.31 | async-start | bytes 163840
  403.2 14.3 collective-permute-start
  417.5 257.7 %copy-start.56 = (bf16[191,512]{1,0:T(8,128)(2,1)}, bf16[191,512]{1,0:T(8,128)(2,1)S(1)}, u32[]{:S(2)}) copy-start(bf16[191,512]{1,0:T(8,128)(2,1)S(1)} %slice.96) | copy-start | bytes 586756
  418.7 256.6 %copy-start.81 = (f32[3,512]{1,0:T(4,128)S(1)}, f32[3,512]{1,0:T(4,128)}, u32[]{:S(2)}) copy-start(f32[3,512]{1,0:T(4,128)} %pad_maximum_fusion) | copy-start | bytes 18436
  1402.1 41.1 %reduce-scatter.48.cloned.1.call-start = ((), (), s32[]{:S(2)}) async-start(), calls=%async_computation.32 | async-start | bytes 163840
  1402.9 64.5 %reduce-scatter.40.cloned.1.call-start = ((), (), s32[]{:S(2)}) async-start(), calls=%async_computation.28 | async-start | bytes 655360
  1405.2 87.0 %reduce-scatter.28.cloned.1.call-start = ((), (), s32[]{:S(2)}) async-start(), calls=%async_computation.22 | async-start | bytes 655360 | tf_op jit(solution)/shard_map/reduce_scatter | solution.py:327
  1405.9 111.0 %reduce-scatter.30.cloned.1.call-start = ((), (), s32[]{:S(2)}) async-start(), calls=%async_computation.23 | async-start | bytes 655360 | tf_op jit(solution)/shard_map/reduce_scatter | solution.py:330
  1406.5 134.5 %reduce-scatter.32.cloned.1.call-start = ((), (), s32[]{:S(2)}) async-start(), calls=%async_computation.24 | async-start | bytes 655360 | tf_op jit(solution)/shard_map/reduce_scatter | solution.py:336
  1407.1 161.9 %reduce-scatter.42.cloned.1.call-start = ((), (), s32[]{:S(2)}) async-start(), calls=%async_computation.29 | async-start | bytes 1310720
  1408.7 188.2 %reduce-scatter.44.cloned.1.call-start = ((), (), s32[]{:S(2)}) async-start(), calls=%async_computation.30 | async-start | bytes 1310720
  1410.2 214.2 %reduce-scatter.38.cloned.1.call-start = ((), (), s32[]{:S(2)}) async-start(), calls=%async_computation.27 | async-start | bytes 1310720 | tf_op jit(solution)/shard_map/reduce_scatter | solution.py:351
  1410.8 247.6 %reduce-scatter.34.cloned.1.call-start = ((), (), s32[]{:S(2)}) async-start(), calls=%async_computation.25 | async-start | bytes 2621440 | tf_op jit(solution)/shard_map/reduce_scatter | solution.py:339
  1411.5 280.8 %reduce-scatter.36.cloned.1.call-start = ((), (), s32[]{:S(2)}) async-start(), calls=%async_computation.26 | async-start | bytes 2621440 | tf_op jit(solution)/shard_map/reduce_scatter | solution.py:345
  (129 other events, 2193.0 us)
Sparse Core Ops, SparseCore 0:
  9.6 19.4 all-gather.9
  30.6 16.7 all-gather.13
  49.0 16.7 all-gather.21
  68.4 60.4 all-gather.11
  131.4 72.0 all-gather.15
  204.9 20.8 all-gather.17
  227.4 22.6 all-gather.19
  402.4 117.9 reduce-scatter.23
  524.0 148.1 reduce-scatter.25
  1402.2 18.3 reduce-scatter.45
  1423.6 19.5 reduce-scatter.47
  1445.7 21.6 reduce-scatter.39
  1470.5 21.6 reduce-scatter.27
  1495.2 21.6 reduce-scatter.29
  1519.3 21.6 reduce-scatter.31
  1544.1 24.8 reduce-scatter.41
  1572.0 24.8 reduce-scatter.43
  1599.4 24.8 reduce-scatter.37
  1626.9 31.3 reduce-scatter.33
  1660.8 31.4 reduce-scatter.35
where the time goes:
time: 1710 us; the launch traced here: 1700 us
  blocking collectives  784 us (46%)
  waiting for transfers between devices  592 us (35%)
  matrix products  137 us (8%)
  local copies, waits for them, and re-layouts  100 us (6%)
  other arithmetic  56.8 us (3%)
  between operations  17.7 us (1%)
    psum x1, blocking collectives, shards(): lax.psum((g_query, g_keyval, g_out, g_cquery, g_ckv, g_cout, g_first, g_b...  726 us
    reduce_scatter x1, waiting for transfers between devices, shards(): lax.psum_scatter(mem_terms, 'ctx', scatter_dimension=0, tiled=True)  149 us
    reduce_scatter x1, waiting for transfers between devices, shards(): lax.psum_scatter(key_terms, 'ctx', scatter_dimension=0, tiled=True)  102 us
    unnamed x25, waiting for transfers between devices  95.2 us
    all_gather x1, waiting for transfers between devices, shards(): mem_all = lax.all_gather(mem_keyvals, 'ctx', axis=0, tiled=True)  37.1 us
  transfers between devices with their start and end apart: 22, of which 17 were waited for; matrix products, arithmetic and copies ran while one was open for 8% of the time, Pallas kernels for 0%

commit v1 on v0

--- a/solution.py
+++ b/solution.py
@@ -235,7 +235,18 @@
     cross_queries = forward_product(hidden_one_low, c_query).astype(jnp.bfloat16)
     mem_rows = memory[0]
     mem_keyvals = forward_product(mem_rows, c_keyval).astype(jnp.bfloat16)
-    mem_all = lax.all_gather(mem_keyvals, "ctx", axis=0, tiled=True)
+    length, mine, extent = (lax.axis_size("ctx"), lax.axis_index("ctx"), mem_keyvals.shape[0])
+    forward = [(i_2, (i_2 + 1) % length) for i_2 in range(length)]
+    out = jnp.zeros(
+        (*mem_keyvals.shape[:0], length * extent, *mem_keyvals.shape[0 + 1 :]), mem_keyvals.dtype
+    )
+    carried_2 = mem_keyvals
+    for lap in range(length):
+        owner = (mine - lap) % length
+        out = lax.dynamic_update_slice_in_dim(out, carried_2, owner * extent, axis=0)
+        if lap < length - 1:
+            carried_2 = lax.ppermute(carried_2, "ctx", forward)
+    mem_all = out
     cross_state = fold_keys(fold_start(n_rows, n_width), cross_queries, mem_all, 0, mem_count)
     cross_mixed, cross_lse = fold_finish(cross_state)
     cross_low = cross_mixed.astype(jnp.bfloat16)

time: 1710 us -> 1740 us (1.018)
  waiting for transfers between devices: 592 us -> 624 us
    ppermute x0 -> x7, waiting for transfers between devices: none -> 86 us  [shards(): carried_2 = lax.ppermute(carried_2, 'ctx', forward)]
    all_gather x1 -> x0, waiting for transfers between devices: 37.1 us -> none  [shards(): mem_all = lax.all_gather(mem_keyvals, 'ctx', axis=0, tiled=True)]
    unnamed x25 -> x24, waiting for transfers between devices: 95.2 us -> 94.6 us
  transfers between devices with their start and end apart: 22 -> 28, of which waited for: 17 -> 20; matrix products, arithmetic and copies ran while one was open for 8% -> 8% of each run, Pallas kernels for 0% -> 0%
where the time goes in v1:
time: 1740 us
  blocking collectives  782 us (45%)
  waiting for transfers between devices  624 us (36%)
  matrix products  140 us (8%)
  local copies, waits for them, and re-layouts  105 us (6%)
  other arithmetic  52.8 us (3%)
    psum x1, blocking collectives, shards(): lax.psum((g_query, g_keyval, g_out, g_cquery, g_ckv, g_cout, g_first, g_b...  726 us
    reduce_scatter x1, waiting for transfers between devices, shards(): lax.psum_scatter(mem_terms, 'ctx', scatter_dimension=0, tiled=True)  149 us
    reduce_scatter x1, waiting for transfers between devices, shards(): lax.psum_scatter(key_terms, 'ctx', scatter_dimension=0, tiled=True)  102 us
    unnamed x24, waiting for transfers between devices  94.6 us
    ppermute x7, waiting for transfers between devices, shards(): carried_2 = lax.ppermute(carried_2, 'ctx', forward)  86 us
  transfers between devices with their start and end apart: 28, of which 20 were waited for; matrix products, arithmetic and copies ran while one was open for 8% of the time, Pallas kernels for 0%

profile of v1, /device:TPU:0, one launch (start us, length us, event | category | flops | bytes accessed | tf_op | source)
XLA Modules:
  0.0 1735.4 jit_solution(3906113417815016289)
XLA Ops:
  9.5 19.6 %all-gather.9.cloned.1.call-done = bf16[512,1024]{1,0:T(8,128)(2,1)} async-done(((bf16[128,1024]{1,0:T(8,128)(2,1)}), bf16[512,1024]{1,0:T(8,128)(2,1)}) %all-gather.9.cloned.1.call-update) | async-done | bytes 1048592 | tf_op jit(solution)/shard_map/all_gather | solution.py:184
  32.2 15.1 all-gather.13.cloned.1.call-done
  52.6 15.3 collective-permute-done
  67.9 19.3 %collective-permute-done.1 = bf16[256,1024]{1,0:T(8,128)(2,1)S(1)} collective-permute-done((bf16[256,1024]{1,0:T(8,128)(2,1)S(1)}, bf16[256,1024]{1,0:T(8,128)(2,1)S(1)}, u32[]{:S(2)}, u32[]{:S(2)}) %collective-permute-start.1) | collective-permute-done | bytes 524320 | tf_op jit(solution)/shard_map/ppermute | solution.py:248
  92.4 15.4 collective-permute-done.2
  122.5 13.0 collective-permute-done.3
  190.3 11.5 collective-permute-done.6
  213.5 27.6 %while.56 = (s32[]{:T(128)}, f32[8,192]{1,0:T(8,128)S(1)}, f32[8,192]{1,0:T(8,128)S(1)}, f32[192,8,64]{0,2,1:T(8,128)}, s32[3]{0:T(128)S(1)}, /*index=5*/s32[]{:...) while((s32[]{:T(128)}, f32[8,192]{1,0:T(8,128)S(1)}, ...), condition=%wide.region_3.4_spmd.clone, body=%wide.region_0.3_spmd.clone.sunk | while | flops 712812544 | bytes 21793044 | solution.py:95
  244.7 36.3 %while.57 = (s32[]{:T(128)}, f32[8,192]{1,0:T(8,128)S(1)}, f32[8,192]{1,0:T(8,128)S(1)}, f32[192,8,64]{0,2,1:T(8,128)}, s32[2]{0:T(128)S(1)}, /*index=5*/s32[]{:...) while((s32[]{:T(128)}, f32[8,192]{1,0:T(8,128)S(1)}, ...), condition=%wide.region_9.10_spmd.clone, body=%wide.region_6.9_spmd.clone.sunk | while | flops 1425320960 | bytes 55611584 | solution.py:95
  302.3 67.4 %while.58 = (s32[]{:T(128)}, f32[192,8,64]{0,2,1:T(8,128)}, f32[2,1024,1024]{2,1,0:T(8,128)}, bf16[2,1024,1024]{1,2,0:T(8,128)(2,1)}, s32[2]{0:T(128)S(1)}, /*in...) while((s32[]{:T(128)}, f32[192,8,64]{0,2,1:T(8,128)}, ...), condition=%wide.region_20.21_spmd.clone, body=%wide.region_19.20_spmd.clone.sunk | while | flops 2029291520 | bytes 105076096 | solution.py:158
  378.5 57.5 %while.59 = (s32[]{:T(128)}, f32[192,8,64]{0,2,1:T(8,128)}, f32[3,512,1024]{2,1,0:T(8,128)}, bf16[3,512,1024]{1,2,0:T(8,128)(2,1)}, s32[3]{0:T(128)S(1)}, /*inde...) while((s32[]{:T(128)}, f32[192,8,64]{0,2,1:T(8,128)}, ...), condition=%wide.region_25.26_spmd.clone, body=%wide.region_24.25_spmd.clone.sunk | while | flops 1014793216 | bytes 47927116 | solution.py:158
  452.7 101.9 %reduce-scatter.24.cloned.1.call-done = f32[192,1024]{1,0:T(8,128)} async-done(((f32[1536,1024]{1,0:T(8,128)}), f32[192,1024]{1,0:T(8,128)}) %reduce-scatter.24.cloned.1.call-update) | async-done | bytes 786448 | tf_op jit(solution)/shard_map/reduce_scatter | solution.py:306
  557.5 148.9 %reduce-scatter.26.cloned.1.call-done = f32[256,1024]{1,0:T(8,128)} async-done(((f32[2048,1024]{1,0:T(8,128)}), f32[256,1024]{1,0:T(8,128)}) %reduce-scatter.26.cloned.1.call-update) | async-done | bytes 1048592 | tf_op jit(solution)/shard_map/reduce_scatter | solution.py:291
  709.4 725.9 %all-reduce.5 = (bf16[512,512]{0,1:T(8,128)(2,1)}, bf16[512,1024]{0,1:T(8,128)(2,1)}, bf16[512,1024]{0,1:T(8,128)(2,1)}, bf16[512,512]{1,0:T(8,128)(2,1)}, bf16[...) all-reduce(f32[512,512]{0,1:T(8,128)} %convolution_bitcast_fusion.2, ...), channel_id=1, replica_groups=mesh['ctx'=8,'wsh'=4] {'ctx'}, use_global_device_ids=true, to_apply=%region_28.29 | all-reduce | flops 4724224 | bytes 28345344 | tf_op jit(solution)/shard_map/psum | solution.py:313
  1464.6 12.6 reduce-scatter.48.cloned.1.call-done
  1478.6 23.0 %reduce-scatter.40.cloned.1.call-done = bf16[128,512]{1,0:T(8,128)(2,1)} async-done(((bf16[512,512]{1,0:T(8,128)(2,1)}), bf16[128,512]{1,0:T(8,128)(2,1)}) %reduce-scatter.40.cloned.1.call-update) | async-done | bytes 131088
  1503.4 22.7 %reduce-scatter.28.cloned.1.call-done = bf16[128,512]{1,0:T(8,128)(2,1)} async-done(((bf16[512,512]{1,0:T(8,128)(2,1)}), bf16[128,512]{1,0:T(8,128)(2,1)}) %reduce-scatter.28.cloned.1.call-update) | async-done | bytes 131088 | tf_op jit(solution)/shard_map/reduce_scatter | solution.py:338
  1527.8 23.3 %reduce-scatter.30.cloned.1.call-done = bf16[128,512]{1,0:T(8,128)(2,1)} async-done(((bf16[512,512]{1,0:T(8,128)(2,1)}), bf16[128,512]{1,0:T(8,128)(2,1)}) %reduce-scatter.30.cloned.1.call-update) | async-done | bytes 131088 | tf_op jit(solution)/shard_map/reduce_scatter | solution.py:341
  1552.7 22.4 %reduce-scatter.32.cloned.1.call-done = bf16[128,512]{1,0:T(8,128)(2,1)} async-done(((bf16[512,512]{1,0:T(8,128)(2,1)}), bf16[128,512]{1,0:T(8,128)(2,1)}) %reduce-scatter.32.cloned.1.call-update) | async-done | bytes 131088 | tf_op jit(solution)/shard_map/reduce_scatter | solution.py:347
  1576.7 26.4 %reduce-scatter.42.cloned.1.call-done = bf16[128,1024]{1,0:T(8,128)(2,1)} async-done(((bf16[512,1024]{1,0:T(8,128)(2,1)}), bf16[128,1024]{1,0:T(8,128)(2,1)}) %reduce-scatter.42.cloned.1.call-update) | async-done | bytes 262160
  1605.2 25.8 %reduce-scatter.44.cloned.1.call-done = bf16[128,1024]{1,0:T(8,128)(2,1)} async-done(((bf16[512,1024]{1,0:T(8,128)(2,1)}), bf16[128,1024]{1,0:T(8,128)(2,1)}) %reduce-scatter.44.cloned.1.call-update) | async-done | bytes 262160
  1633.1 25.4 %reduce-scatter.38.cloned.1.call-done = bf16[256,512]{1,0:T(8,128)(2,1)} async-done(((bf16[1024,512]{1,0:T(8,128)(2,1)}), bf16[256,512]{1,0:T(8,128)(2,1)}) %reduce-scatter.38.cloned.1.call-update) | async-done | bytes 262160 | tf_op jit(solution)/shard_map/reduce_scatter | solution.py:362
  1660.3 32.0 %reduce-scatter.34.cloned.1.call-done = bf16[128,2048]{1,0:T(8,128)(2,1)} async-done(((bf16[512,2048]{1,0:T(8,128)(2,1)}), bf16[128,2048]{1,0:T(8,128)(2,1)}) %reduce-scatter.34.cloned.1.call-update) | async-done | bytes 524304 | tf_op jit(solution)/shard_map/reduce_scatter | solution.py:350
  1694.4 32.0 %reduce-scatter.36.cloned.1.call-done = bf16[512,512]{1,0:T(8,128)(2,1)} async-done(((bf16[2048,512]{1,0:T(8,128)(2,1)}), bf16[512,512]{1,0:T(8,128)(2,1)}) %reduce-scatter.36.cloned.1.call-update) | async-done | bytes 524304 | tf_op jit(solution)/shard_map/reduce_scatter | solution.py:356
  (540 shorter events, 378.8 us)
Async XLA Ops:
  7.2 21.9 %all-gather.9.cloned.1.call-start = ((), (), s32[]{:S(2)}) async-start(), calls=%async_computation.13 | async-start | bytes 1310720 | tf_op jit(solution)/shard_map/all_gather | solution.py:184
  7.9 39.4 %all-gather.13.cloned.1.call-start = ((), (), s32[]{:S(2)}) async-start(), calls=%async_computation.15 | async-start | bytes 1310720 | tf_op jit(solution)/shard_map/all_gather | solution.py:187
  8.7 169.9 %all-gather.19.cloned.1.call-start = ((), (), s32[]{:S(2)}) async-start(), calls=%async_computation.18 | async-start | bytes 1310720 | tf_op jit(solution)/shard_map/all_gather | solution.py:193
  9.4 199.4 %all-gather.11.cloned.1.call-start = ((), (), s32[]{:S(2)}) async-start(), calls=%async_computation.14 | async-start | bytes 3538944 | tf_op jit(solution)/shard_map/all_gather | solution.py:226
  31.5 251.3 %all-gather.15.cloned.1.call-start = ((), (), s32[]{:S(2)}) async-start(), calls=%async_computation.16 | async-start | bytes 2621440 | tf_op jit(solution)/shard_map/all_gather | solution.py:189
  32.1 254.1 %all-gather.17.cloned.1.call-start = ((), (), s32[]{:S(2)}) async-start(), calls=%async_computation.17 | async-start | bytes 2621440 | tf_op jit(solution)/shard_map/all_gather | solution.py:191
  87.3 20.5 %collective-permute-start.2 = (bf16[256,1024]{1,0:T(8,128)(2,1)S(1)}, bf16[256,1024]{1,0:T(8,128)(2,1)S(1)}, u32[]{:S(2)}, u32[]{:S(2)}) collective-permute-start(bf16[256,1024]{1,0:T(8,128)(2,1)S(1)} %collective-permute-done.1), channel_id=1, source_target_pairs={{0,4},{4,8},{8,12},{12,16},{16,20},{20,24},{24,28},{28,0},{1,5},{5... | collective-permute-start | bytes 1572872 | tf_op jit(solution)/shard_map/ppermute | solution.py:248
  87.3 467.3 %reduce-scatter.24.cloned.1.call-start = ((), (), s32[]{:S(2)}) async-start(), calls=%async_computation.19 | async-start | bytes 7077888 | tf_op jit(solution)/shard_map/reduce_scatter | solution.py:306
  107.8 27.7 %collective-permute-start.3 = (bf16[256,1024]{1,0:T(8,128)(2,1)S(1)}, bf16[256,1024]{1,0:T(8,128)(2,1)S(1)}, u32[]{:S(2)}, u32[]{:S(2)}) collective-permute-start(bf16[256,1024]{1,0:T(8,128)(2,1)S(1)} %collective-permute-done.2), channel_id=1, source_target_pairs={{0,4},{4,8},{8,12},{12,16},{16,20},{20,24},{24,28},{28,0},{1,5},{5... | collective-permute-start | bytes 1572872 | tf_op jit(solution)/shard_map/ppermute | solution.py:248
  135.6 23.3 %collective-permute-start.4 = (bf16[256,1024]{1,0:T(8,128)(2,1)S(1)}, bf16[256,1024]{1,0:T(8,128)(2,1)}, u32[]{:S(2)}, u32[]{:S(2)}) collective-permute-start(bf16[256,1024]{1,0:T(8,128)(2,1)S(1)} %collective-permute-done.3), channel_id=1, source_target_pairs={{0,4},{4,8},{8,12},{12,16},{16,20},{20,24},{24,28},{28,0},{1,5},{5... | collective-permute-start | bytes 1572872 | tf_op jit(solution)/shard_map/ppermute | solution.py:248
  158.8 24.6 %collective-permute-start.5 = (bf16[256,1024]{1,0:T(8,128)(2,1)}, bf16[256,1024]{1,0:T(8,128)(2,1)}, u32[]{:S(2)}, u32[]{:S(2)}) collective-permute-start(bf16[256,1024]{1,0:T(8,128)(2,1)} %collective-permute-done.4), channel_id=1, source_target_pairs={{0,4},{4,8},{8,12},{12,16},{16,20},{20,24},{24,28},{28,0},{1,5},{5... | collective-permute-start | bytes 1572872 | tf_op jit(solution)/shard_map/ppermute | solution.py:248
  181.3 109.2 %collective-permute-start.8 = (f32[1,512]{1,0:T(1,128)S(1)}, f32[1,512]{1,0:T(1,128)S(1)}, u32[]{:S(2)}, u32[]{:S(2)}) collective-permute-start(f32[1,512]{1,0:T(1,128)S(1)} %slice.99), channel_id=1, source_target_pairs={{0,4},{4,8},{8,12},{12,16},{16,20},{20,24},{24,28},{1,5},{5,9},{9,... | collective-permute-start | bytes 6152 | tf_op jit(solution)/shard_map/ppermute | solution.py:16
  436.1 270.3 %reduce-scatter.26.cloned.1.call-start = ((), (), s32[]{:S(2)}) async-start(), calls=%async_computation.20 | async-start | bytes 9437184 | tf_op jit(solution)/shard_map/reduce_scatter | solution.py:291
  436.9 1026.3 %reduce-scatter.46.cloned.1.call-start = ((), (), s32[]{:S(2)}) async-start(), calls=%async_computation.30 | async-start | bytes 163840
  1436.2 41.0 %reduce-scatter.48.cloned.1.call-start = ((), (), s32[]{:S(2)}) async-start(), calls=%async_computation.31 | async-start | bytes 163840
  1437.0 64.5 %reduce-scatter.40.cloned.1.call-start = ((), (), s32[]{:S(2)}) async-start(), calls=%async_computation.27 | async-start | bytes 655360
  1439.3 86.9 %reduce-scatter.28.cloned.1.call-start = ((), (), s32[]{:S(2)}) async-start(), calls=%async_computation.21 | async-start | bytes 655360 | tf_op jit(solution)/shard_map/reduce_scatter | solution.py:338
  1439.8 111.2 %reduce-scatter.30.cloned.1.call-start = ((), (), s32[]{:S(2)}) async-start(), calls=%async_computation.22 | async-start | bytes 655360 | tf_op jit(solution)/shard_map/reduce_scatter | solution.py:341
  1440.6 134.5 %reduce-scatter.32.cloned.1.call-start = ((), (), s32[]{:S(2)}) async-start(), calls=%async_computation.23 | async-start | bytes 655360 | tf_op jit(solution)/shard_map/reduce_scatter | solution.py:347
  1441.2 162.0 %reduce-scatter.42.cloned.1.call-start = ((), (), s32[]{:S(2)}) async-start(), calls=%async_computation.28 | async-start | bytes 1310720
  1442.8 188.2 %reduce-scatter.44.cloned.1.call-start = ((), (), s32[]{:S(2)}) async-start(), calls=%async_computation.29 | async-start | bytes 1310720
  1444.2 214.3 %reduce-scatter.38.cloned.1.call-start = ((), (), s32[]{:S(2)}) async-start(), calls=%async_computation.26 | async-start | bytes 1310720 | tf_op jit(solution)/shard_map/reduce_scatter | solution.py:362
  1444.8 247.4 %reduce-scatter.34.cloned.1.call-start = ((), (), s32[]{:S(2)}) async-start(), calls=%async_computation.24 | async-start | bytes 2621440 | tf_op jit(solution)/shard_map/reduce_scatter | solution.py:350
  1445.4 281.0 %reduce-scatter.36.cloned.1.call-start = ((), (), s32[]{:S(2)}) async-start(), calls=%async_computation.25 | async-start | bytes 2621440 | tf_op jit(solution)/shard_map/reduce_scatter | solution.py:356
  (125 other events, 3356.0 us)
Sparse Core Ops, SparseCore 0:
  9.6 19.4 all-gather.8
  30.6 16.7 all-gather.12
  48.9 16.7 all-gather.18
  68.3 80.3 all-gather.10
  150.2 27.7 all-gather.14
  179.4 23.3 all-gather.16
  436.2 118.3 reduce-scatter.23
  558.2 148.1 reduce-scatter.25
  1436.3 18.3 reduce-scatter.45
  1457.5 19.5 reduce-scatter.47
  1479.8 21.6 reduce-scatter.39
  1504.4 21.6 reduce-scatter.27
  1529.3 21.6 reduce-scatter.29
  1553.4 21.6 reduce-scatter.31
  1578.2 24.8 reduce-scatter.41
  1606.1 24.8 reduce-scatter.43
  1633.6 24.8 reduce-scatter.37
  1660.9 31.3 reduce-scatter.33
  1695.0 31.4 reduce-scatter.35
